TPU v7x, 128 devices: a whole 4x4x4 slice. The times are simulated.
128 devices in a mesh: facet: 32 (over z, y_hi, x), freq: 4 (over y_lo, core).
Axes of the slice: x: 4, y: 4 (y_hi: 2, y_lo: 2; y = y_hi * 2 + y_lo), z: 4, core: 2. Of those that a mesh axis runs over, the one named last changes fastest.
Arguments:
- visibilities: float32 [32, 10, 2, 128, 128], P('facet', None, None, 'freq'), may hold values from -6 to 6
- coords: float32 [32, 10, 3, 128], P('facet'), may hold values from -1500 to 1500, as said below
- corners: int32 [2, 32, 10], replicated, may hold values from 0 to 480
- owners: int32 [2], replicated, may hold values from 0 to 31, as said below
- assign: int32 [32, 20], P('facet'), may hold values from 0 to 19, as said below
- counts: int32 [32], P('facet'), may hold values from 2 to 20, as said below
Outputs:
- dirty: float32 [32, 512, 512], P('facet', 'freq')
Inputs may be any that keep to these rules, and one draw needn't show every extreme that they name: `owners`: the two sets lie in different slots, one of them in the last slot. `assign`: each facet's row is a permutation of the 20 block numbers; only its first counts entries are gridded. `counts`: some facet grids all 20 blocks. `coords`: at every channel, u and v of each row of a block lie within 12 cells of the centre of that block's subgrid.
All inputs are finite; a program needn't handle non-finite values.
Results may differ from a plain program's by a relative error of at most 0.0037.
Values sent between devices are 32-bit elements; how exact they have to be, the bound alone decides.
A program may use at most 64 MiB of HBM per device.

v0:
```python
import math

import jax
import jax.numpy as jnp
from jax import lax
from jax.sharding import PartitionSpec as P

SUB = 32
G = 512


two_pi = 2.0 * math.pi
field_width = 0.02
band_spread = 0.02
batch_items = 8
highest = lax.Precision.HIGHEST


def spread(value, axis, source):
    kept = jnp.where(lax.axis_index(axis) == source, value, 0).astype(value.dtype)
    return lax.psum(kept, axis)


def facet_center(facet_id, facet_total):
    row_total = facet_total // 8
    column = (facet_id % 8).astype(jnp.float32) - 3.5
    row_pos = (facet_id // 8).astype(jnp.float32) - (row_total - 1) / 2.0
    radius = field_width * field_width * (column * column + row_pos * row_pos)
    w_shift = -radius / (1.0 + jnp.sqrt(1.0 - radius))
    return (column, row_pos, w_shift)


def subgrid_tables():
    offsets = jnp.arange(SUB, dtype=jnp.int32) - SUB // 2
    position = offsets.astype(jnp.float32)
    profile = 1.0 - 0.8 * (position / (SUB / 2.0)) ** 2
    taper_square = profile[:, None] * profile[None, :]
    phase_index = offsets[:, None] * offsets[None, :] % SUB
    phase_angle = -two_pi * phase_index.astype(jnp.float32) / SUB
    return (position, taper_square, jnp.cos(phase_angle), jnp.sin(phase_angle))


def image_tables():
    offsets = jnp.arange(G, dtype=jnp.int32) - G // 2
    phase_index = offsets[:, None] * offsets[None, :] % G
    phase_angle = two_pi * phase_index.astype(jnp.float32) / G
    return (jnp.cos(phase_angle), jnp.sin(phase_angle))


def subgrid_terms(
    vis_blocks, coord_blocks, freq_ratio, corner_u, corner_v, column, row_pos, w_shift, tables
):
    position = tables[0]
    item_total = vis_blocks.shape[0]
    scaled = coord_blocks[:, :, None, :] * freq_ratio[None, None, :, None]
    u_cells = scaled[:, 0]
    v_cells = scaled[:, 1]
    w_waves = scaled[:, 2]
    rotation = two_pi * (
        u_cells * column[:, None, None]
        + v_cells * row_pos[:, None, None]
        + w_waves * w_shift[:, None, None]
    )
    rot_real = jnp.cos(rotation)
    rot_imag = jnp.sin(rotation)
    vis_real = vis_blocks[:, 0] * rot_real - vis_blocks[:, 1] * rot_imag
    vis_imag = vis_blocks[:, 0] * rot_imag + vis_blocks[:, 1] * rot_real
    centre_shift = G // 2 - SUB // 2
    delta_u = (u_cells + (centre_shift - corner_u).astype(jnp.float32)[:, None, None]).reshape(
        item_total, 1, -1
    )
    delta_v = (v_cells + (centre_shift - corner_v).astype(jnp.float32)[:, None, None]).reshape(
        item_total, 1, -1
    )
    angle_u = two_pi / SUB * delta_u * position[None, :, None]
    left_factor = jnp.concatenate([jnp.cos(angle_u), jnp.sin(angle_u)], axis=2).astype(jnp.bfloat16)
    angle_v = two_pi / SUB * delta_v * position[None, :, None]
    wave_real = jnp.cos(angle_v)
    wave_imag = jnp.sin(angle_v)
    flat_real = vis_real.reshape(item_total, 1, -1)
    flat_imag = vis_imag.reshape(item_total, 1, -1)
    right_real = flat_real * wave_real - flat_imag * wave_imag
    right_imag = flat_real * wave_imag + flat_imag * wave_real
    upper_rows = jnp.concatenate([right_real, -right_imag], axis=2)
    lower_rows = jnp.concatenate([right_imag, right_real], axis=2)
    right_factor = jnp.concatenate([upper_rows, lower_rows], axis=1).astype(jnp.bfloat16)
    return (left_factor, right_factor)


def subgrid_finish(product, tables):
    taper_square, dft_real, dft_imag = (tables[1], tables[2], tables[3])
    image_real = product[:, :, :SUB] * taper_square
    image_imag = product[:, :, SUB:] * taper_square
    half_real = jnp.einsum("pl,slm->spm", dft_real, image_real, precision=highest) - jnp.einsum(
        "pl,slm->spm", dft_imag, image_imag, precision=highest
    )
    half_imag = jnp.einsum("pl,slm->spm", dft_real, image_imag, precision=highest) + jnp.einsum(
        "pl,slm->spm", dft_imag, image_real, precision=highest
    )
    uv_real = jnp.einsum("spm,qm->spq", half_real, dft_real, precision=highest) - jnp.einsum(
        "spm,qm->spq", half_imag, dft_imag, precision=highest
    )
    uv_imag = jnp.einsum("spm,qm->spq", half_real, dft_imag, precision=highest) + jnp.einsum(
        "spm,qm->spq", half_imag, dft_real, precision=highest
    )
    return jnp.stack([uv_real, uv_imag], axis=1)


def add_pieces(uv_grid, pieces, corner_u, corner_v, weights):
    zero_index = jnp.zeros((), jnp.int32)
    for item in range(batch_items):
        anchor = (zero_index, corner_u[item], corner_v[item])
        current = lax.dynamic_slice(uv_grid, anchor, (2, SUB, SUB))
        uv_grid = lax.dynamic_update_slice(uv_grid, current + pieces[item] * weights[item], anchor)
    return uv_grid


def broadcast_set(visibilities, coords, set_owner):
    return (spread(visibilities, "facet", set_owner), spread(coords, "facet", set_owner))


def grid_items(block_data, list_pair, end_item, count_first, centre_pair, freq_ratio, tables):
    vis_all, coord_all, corner_all = block_data
    first_list, second_list = list_pair
    first_centre, second_centre = centre_pair
    list_length = first_list.shape[0]

    def grid_step(batch_index, grid_pair):
        item_index = batch_index * batch_items + jnp.arange(batch_items, dtype=jnp.int32)
        is_live = item_index < end_item
        is_later = item_index >= count_first
        slot_index = jnp.clip(
            jnp.where(is_later, item_index - count_first, item_index), 0, list_length - 1
        )
        block_index = jnp.where(
            is_later, jnp.take(second_list, slot_index), jnp.take(first_list, slot_index)
        )
        column = jnp.where(is_later, second_centre[0], first_centre[0])
        row_pos = jnp.where(is_later, second_centre[1], first_centre[1])
        w_shift = jnp.where(is_later, second_centre[2], first_centre[2])
        corner_u = jnp.take(corner_all[0], block_index)
        corner_v = jnp.take(corner_all[1], block_index)
        left_factor, right_factor = subgrid_terms(
            jnp.take(vis_all, block_index, axis=0),
            jnp.take(coord_all, block_index, axis=0),
            freq_ratio,
            corner_u,
            corner_v,
            column,
            row_pos,
            w_shift,
            tables,
        )
        product = jnp.einsum(
            "slk,smk->slm", left_factor, right_factor, preferred_element_type=jnp.float32
        )
        pieces = subgrid_finish(product, tables)
        first_weight = jnp.logical_and(is_live, jnp.logical_not(is_later)).astype(jnp.float32)
        return (add_pieces(grid_pair[0], pieces, corner_u, corner_v, first_weight),)

    empty_grid = jnp.zeros((2, G, G), jnp.float32)
    initial = (empty_grid,)
    batch_total = (end_item + batch_items - 1) // batch_items
    return lax.fori_loop(0, batch_total, grid_step, initial)


def on_device(visibilities, coords, corners, owners, assign, counts):
    facet_total = lax.axis_size("facet")
    band_total = lax.axis_size("freq")
    facet_index = lax.axis_index("facet")
    band_index = lax.axis_index("freq")
    local_channels = visibilities.shape[3]
    block_count = visibilities.shape[1]
    block_rows = visibilities.shape[4]
    channel_total = local_channels * band_total
    channel = band_index * local_channels + jnp.arange(local_channels, dtype=jnp.int32)
    freq_ratio = 1.0 + band_spread * channel.astype(jnp.float32) / channel_total
    first_vis, first_coords = broadcast_set(visibilities, coords, owners[0])
    second_vis, second_coords = broadcast_set(visibilities, coords, owners[1])
    vis_all = jnp.concatenate([first_vis, second_vis], axis=0).reshape(
        2 * block_count, 2, local_channels, block_rows
    )
    coord_all = jnp.concatenate([first_coords, second_coords], axis=0).reshape(
        2 * block_count, 3, block_rows
    )
    corner_all = jnp.take(corners, owners, axis=1).reshape(2, 2 * block_count)
    block_data = (vis_all, coord_all, corner_all)
    tables = subgrid_tables()
    own_list = assign[0]
    own_count = counts[0]
    own_centre = facet_center(facet_index, facet_total)
    (uv_grid,) = grid_items(
        block_data,
        (own_list, own_list),
        own_count,
        own_count,
        (own_centre, own_centre),
        freq_ratio,
        tables,
    )
    cos_table, sin_table = image_tables()
    image_scale = 1.0 / (SUB * SUB * math.sqrt(2 * block_count * block_rows * channel_total))
    right_real = jnp.dot(
        uv_grid[0], cos_table, precision=highest, preferred_element_type=jnp.float32
    ) - jnp.dot(uv_grid[1], sin_table, precision=highest, preferred_element_type=jnp.float32)
    right_imag = jnp.dot(
        uv_grid[0], sin_table, precision=highest, preferred_element_type=jnp.float32
    ) + jnp.dot(uv_grid[1], cos_table, precision=highest, preferred_element_type=jnp.float32)
    image_part = lax.psum_scatter(
        (
            jnp.dot(cos_table, right_real, precision=highest, preferred_element_type=jnp.float32)
            - jnp.dot(sin_table, right_imag, precision=highest, preferred_element_type=jnp.float32)
        )
        * image_scale,
        "freq",
        scatter_dimension=0,
        tiled=True,
    )
    return image_part[None]


def solution(mesh):
    placed = (
        P("facet", None, None, "freq", None),
        P("facet", None, None, None),
        P(),
        P(),
        P("facet", None),
        P("facet"),
    )
    return jax.shard_map(
        on_device, mesh=mesh, in_specs=placed, out_specs=P("facet", "freq", None), check_vma=False
    )
```

profile of v0, /device:TPU:1, one launch (start us, length us, event | category | flops | bytes accessed | tf_op | source)
XLA Modules:
  0.0 707.3 jit_solution(16114662937613344052)
XLA Ops:
  6.5 1.4 fusion.197
  9.3 1.9 broadcast_select_fusion.5
  11.9 0.7 compare_select_fusion.3
  12.6 0.7 compare_and_fusion.1
  13.3 0.7 broadcast_select_fusion.7
  14.1 159.7 %all-reduce = (f32[1,10,3,128]{3,0,2,1:T(1,128)S(1)}, f32[1,10,3,128]{3,0,2,1:T(1,128)S(1)}) all-reduce(f32[1,10,3,128]{3,0,2,1:T(1,128)S(1)} %get-tuple-element.335, f32[1,10,3,128]{3,0,2,1:T(1,128)S(1)} %get-tuple-element.334), channel_id=1, replica_groups=mesh['facet'=32,'freq'=4] {'facet'}, use_global_device_ids=true, to_apply=%region_3.4 | all-reduce | flops 7680 | bytes 61440 | tf_op jit(solution)/shard_map/psum | solution.py:21
  173.8 0.6 copy.43
  174.5 0.8 copy.41
  177.9 161.6 %all-reduce.4.cloned.1.call-done = (f32[1,10,2,32,128]{4,3,2,1,0:T(8,128)}, f32[1,10,2,32,128]{4,3,2,1,0:T(8,128)}) async-done(((f32[1,10,2,32,128]{4,3,2,1,0:T(8,128)}, f32[1,10,2,32,128]{4,3,2,1,0:T(8,128)}), (f32[1,10,2,32,128]{4,3,2,1,0:T(8,128)}, f32[1,10,2,32,128]{4,3,2,1,0:T(8,128)})) %all-reduce.4.cloned.1.call-update) | async-done | bytes 655376 | tf_op jit(solution)/shard_map/psum | solution.py:21
  339.5 1.1 pad_maximum_fusion.1
  340.9 95.7 %while.13 = (s32[]{:T(128)}, f32[2,512,512]{2,1,0:T(8,128)S(1)}, s32[]{:T(128)}, s32[2,20]{1,0:T(2,128)}, s32[]{:T(128)}, /*index=5*/s32[20]{0:T(128)S(1)}, f32[...) while((s32[]{:T(128)}, f32[2,512,512]{2,1,0:T(8,128)S(1)}, ...), condition=%wide.region_5.7_spmd.clone.clone.clone, body=%wide.region_4.6_spmd.clone.clone.clone.sunk | while | flops 351148544 | bytes 27451300 | solution.py:164
  341.0 0.7 compare_select_fusion.6
  341.6 0.6 gather_fusion
  342.3 0.7 compare_and_fusion.3
  343.0 0.8 slice_bitcast_fusion.8
  343.7 0.6 gather_fusion.2
  344.4 0.6 gather_fusion.3
  345.0 1.4 gather_fusion.1
  347.1 0.7 gather_fusion.4
  347.8 0.8 broadcast_select_fusion.14
  349.1 31.2 %fusion.257 = (bf16[8,32,4096]{2,1,0:T(8,128)(2,1)S(1)}, bf16[8,32,4096]{2,1,0:T(8,128)(2,1)S(1)}, bf16[8,32,4096]{2,1,0:T(8,128)(2,1)S(1)}, bf16[8,32,4096]{2,1,0:T(8,128)(2,1)S(1)}, bf16[8,32,4096]{2,1,0:T(8,128)(2,1)S(1)}) fusion(f32[32]{0:T(128)S(1)} %add_convert_fusion.2, f32[8,4096]{1,0:T(8,128)S(1)} %get-tuple-element.475, ...), kind=kLoop, calls=%fused_computation.33.clone.1 | loop fusion | flops 14680064 | bytes 11010176 | tf_op jit(solution)/shard_map/convert.6
  380.3 3.3 fusion.258
  387.4 0.7 fusion.267
  391.7 0.7 fusion.268
  392.4 0.7 fusion.269
  393.0 0.7 fusion.270
  393.7 1.2 dynamic_update_slice.56
  398.8 0.7 fusion.271
  399.5 1.4 dynamic_update_slice.57
  404.8 0.8 fusion.272
  405.6 1.4 dynamic_update_slice.58
  410.7 0.8 fusion.273
  411.5 1.2 dynamic_update_slice.59
  416.6 0.6 fusion.274
  417.3 1.4 dynamic_update_slice.60
  422.4 0.7 fusion.275
  423.1 1.4 dynamic_update_slice.61
  428.1 0.7 fusion.276
  428.8 1.4 dynamic_update_slice.62
  434.4 0.7 fusion.277
  435.0 1.4 dynamic_update_slice.63
  436.6 6.5 fusion.151
  443.1 5.7 fusion.153
  448.9 5.9 convolution_add_fusion.2
  454.8 5.8 convolution_subtract_fusion.3
  460.6 5.9 fusion.162
  466.5 7.0 fusion.145
  473.5 226.5 %reduce-scatter.2.cloned.1.call-done = f32[128,512]{1,0:T(8,128)} async-done(((f32[512,512]{1,0:T(8,128)}), f32[128,512]{1,0:T(8,128)}) %reduce-scatter.2.cloned.1.call-update) | async-done | bytes 262160 | tf_op jit(solution)/shard_map/reduce_scatter | solution.py:209
  (46 shorter events, 7.9 us)
Async XLA Ops:
  6.5 333.0 %all-reduce.4.cloned.1.call-start = ((), (), s32[]{:S(2)}) async-start(), calls=%async_computation.2 | async-start | bytes 1310720 | tf_op jit(solution)/shard_map/psum | solution.py:21
  11.2 329.8 %copy-start = (s32[1,20]{1,0:T(1,128)S(1)}, s32[1,20]{1,0:T(1,128)}, u32[]{:S(2)}) copy-start(s32[1,20]{1,0:T(1,128)} %param.14) | copy-start | bytes 244
  11.2 688.9 %reduce-scatter.2.cloned.1.call-start = ((), (), s32[]{:S(2)}) async-start(), calls=%async_computation.1 | async-start | bytes 1310720 | tf_op jit(solution)/shard_map/reduce_scatter | solution.py:209
  343.0 3.7 copy-start.2
  343.0 3.4 copy-start.1
  380.3 3.3 copy-start.3
  436.6 6.5 copy-start.4
Sparse Core Ops, SparseCore 0:
  11.3 328.1 all-reduce.3
  473.7 226.3 reduce-scatter.1
where the time goes:
time: 719 us; the launch traced here: 707 us
  waiting for transfers between devices  388 us (54%)
  blocking collectives  160 us (22%)
  other arithmetic  47.7 us (7%)
  matrix products  43.7 us (6%)
  loops' own time  31 us (4%)
  local copies, waits for them, and re-layouts  20.8 us (3%)
  between operations  16.1 us (2%)
    reduce_scatter x1, waiting for transfers between devices, on_device(): lax.psum_scatter((jnp.dot(cos_table, right_real, precision=highest, prefe...  227 us
    psum x1, waiting for transfers between devices, spread(): return lax.psum(kept, axis)  162 us
    psum x1, blocking collectives, spread(): return lax.psum(kept, axis)  160 us
    another operation x1, other arithmetic  31.2 us
    another operation x1, loops' own time, grid_items(): return lax.fori_loop(0, batch_total, grid_step, initial)  31 us
  transfers between devices with their start and end apart: 2, of which 2 were waited for; matrix products, arithmetic and copies ran while one was open for 1% of the time, Pallas kernels for 0%

commit v1 on v0

v1 whole, which is shorter than its diff:
```python
import functools
import math

import jax
import jax.numpy as jnp
import numpy as np
from jax import lax
from jax.experimental import pallas as pl
from jax.experimental.pallas import tpu as pltpu
from jax.sharding import PartitionSpec as P

SUB = 32
G = 512
BPC = 10
CH = 32
N_FACET = 32
N_FREQ = 4
BLK = 128
CHANS = CH * N_FREQ
CHUNK = 8
MESH = pl.DeviceIdType.MESH
f32 = jnp.float32
bf16 = jnp.bfloat16

DELTA = (
    (0, 0, 0),
    (1, 0, 0),
    (3, 0, 0),
    (0, 0, 1),
    (0, 0, 3),
    (1, 0, 1),
    (1, 0, 3),
    (3, 0, 1),
    (3, 0, 3),
    (0, 1, 0),
)
LAST = N_FACET - 1
SLOTS = 11


def fit_sincos():
    s = 0.125 * (1.0 - np.cos(np.pi * (np.arange(400) + 0.5) / 400))
    t = np.sqrt(s)
    poly = np.polynomial.chebyshev
    domain = [0.0, 0.25]
    c = poly.Chebyshev.fit(s, np.cos(2 * np.pi * t), 7, domain=domain)
    n = poly.Chebyshev.fit(s, np.sin(2 * np.pi * t) / t, 7, domain=domain)
    to_power = lambda p: p.convert(kind=np.polynomial.Polynomial).coef
    return [float(v) for v in to_power(c)], [float(v) for v in to_power(n)]


COS_POLY, SIN_POLY = fit_sincos()


def sincos(cycles):
    t = cycles - jnp.floor(cycles + 0.5)
    s = t * t
    c = jnp.full_like(s, COS_POLY[-1])
    for k in COS_POLY[-2::-1]:
        c = c * s + k
    n = jnp.full_like(s, SIN_POLY[-1])
    for k in SIN_POLY[-2::-1]:
        n = n * s + k
    return c, n * t


def cmul(a, b):
    return a[0] * b[0] - a[1] * b[1], a[0] * b[1] + a[1] * b[0]


def both(a, b):
    rr, ii, ri, ir = a[0] * b[0], a[1] * b[1], a[0] * b[1], a[1] * b[0]
    return (rr - ii, ri + ir), (rr + ii, ir - ri)


def image_table():
    x = np.arange(G) - G // 2
    l = np.arange(SUB) - SUB // 2
    n = np.arange(SUB) - SUB // 2
    theta = x[:, None] / G - l[None, :] / SUB
    kernel = np.exp(2j * np.pi * n[None, None, :] * theta[:, :, None]).sum(axis=2)
    real = (kernel * np.exp(1j * np.pi * theta)).real
    real = real * (1.0 - 0.8 * (l / (SUB / 2.0)) ** 2)[None, :]
    upper, lower = real[:, SUB // 2 :], real[:, SUB // 2 - 1 :: -1]
    return np.concatenate([upper + lower, upper - lower], axis=1)


def shifted(f, delta, sign):
    z, y, x = f // 8, (f // 4) % 2, f % 4
    z = (z + (delta[0] if sign > 0 else 4 - delta[0])) % 4
    y = (y + delta[1]) % 2
    x = (x + (delta[2] if sign > 0 else 4 - delta[2])) % 4
    return z * 8 + y * 4 + x


def shifted_int(f, delta):
    return ((f // 8 + delta[0]) % 4) * 8 + ((f // 4 % 2 + delta[1]) % 2) * 4 + (f % 4 + delta[2]) % 4


LAST_POS = tuple(shifted_int(LAST, d) for d in DELTA)


def exchange_kernel(vis, coord, cand_vis, cand_coord, send_sem, recv_sem):
    f = lax.axis_index("facet")
    q = lax.axis_index("freq")
    barrier = pltpu.get_barrier_semaphore()
    for j in range(1, BPC):
        pl.semaphore_signal(
            barrier, inc=1, device_id=(shifted(f, DELTA[j], -1), q), device_id_type=MESH
        )
    own = [
        pltpu.make_async_copy(vis.at[0, 0], cand_vis.at[0], recv_sem.at[0, 0]),
        pltpu.make_async_copy(coord.at[0, 0], cand_coord.at[0], recv_sem.at[0, 1]),
    ]
    for c in own:
        c.start()
    pl.semaphore_wait(barrier, BPC - 1)
    copies = []
    for j in range(BPC - 1, 0, -1):
        to = (shifted(f, DELTA[j], 1), q)
        for n, (src, dst) in enumerate(((vis, cand_vis), (coord, cand_coord))):
            copies.append(
                pltpu.make_async_remote_copy(
                    src_ref=src.at[0, j],
                    dst_ref=dst.at[j],
                    send_sem=send_sem.at[j, n],
                    recv_sem=recv_sem.at[j, n],
                    device_id=to,
                    device_id_type=MESH,
                )
            )
            copies[-1].start()
    for c in own:
        c.wait()
    for c in copies:
        c.wait()


def exchange(vis, coord):
    return pl.pallas_call(
        exchange_kernel,
        out_shape=(
            jax.ShapeDtypeStruct((BPC, 2, CH, BLK), f32),
            jax.ShapeDtypeStruct((BPC, 3, BLK), f32),
        ),
        in_specs=[pl.BlockSpec(memory_space=pl.ANY)] * 2,
        out_specs=[pl.BlockSpec(memory_space=pl.ANY)] * 2,
        scratch_shapes=[
            pltpu.SemaphoreType.DMA((BPC, 2)),
            pltpu.SemaphoreType.DMA((BPC, 2)),
        ],
        compiler_params=pltpu.CompilerParams(collective_id=0, has_side_effects=True),
        name="exchange_blocks",
    )(vis, coord)


def prepare_unit(q, vis, coord, ou, ov, xs, ys, vs):
    channel = q * CH + lax.broadcasted_iota(jnp.int32, (CH, BLK), 0)
    ratio = 1.0 + 0.02 * channel.astype(f32) / CHANS
    u = coord[0:1, :] * ratio
    v = coord[1:2, :] * ratio
    w = coord[2:3, :] * ratio
    du = u + (240.5 - ou.astype(f32))
    dv = v + (240.5 - ov.astype(f32))
    zeta = []
    for d, ref in ((du, xs), (dv, ys)):
        base = sincos(d * (1.0 / 64.0))
        zeta.append(base)
        square = cmul(base, base)
        powers = [base]
        while len(powers) < 16:
            powers += [cmul(p, square) for p in powers]
            square = cmul(square, square)
        for i, (c, s) in enumerate(powers):
            ref[i * CH : (i + 1) * CH, :] = c
            ref[(i + 16) * CH : (i + 17) * CH, :] = s
    turn = cmul(zeta[0], zeta[1])
    value = cmul((vis[0], vis[1]), (turn[0], -turn[1]))
    pu = sincos(u * 0.5)
    pu2 = cmul(pu, pu)
    a_phase = [pu]
    for _ in range(3):
        a_phase.append(cmul(a_phase[-1], pu2))
    pv = sincos(v * 0.5)
    e_phase = [pv, cmul(pv, cmul(pv, pv))]
    for e in range(2):
        plus, minus = both(value, e_phase[e])
        for a in range(4):
            rho = 0.0004 * ((a + 0.5) ** 2 + (e + 0.5) ** 2)
            depth = sincos(w * (-rho / (1.0 + math.sqrt(1.0 - rho))))
            for row, turned in ((2 + e, plus), (1 - e, minus)):
                right, left = both(cmul(turned, depth), a_phase[a])
                for column, out in ((4 + a, right), (3 - a, left)):
                    facet = row * 8 + column
                    vs[facet * CH : (facet + 1) * CH, :] = out[0]
                    vs[(facet + 32) * CH : (facet + 33) * CH, :] = out[1]


def unit_products(xs, ys, vs, pbuf, vbuf, acc, turned, put):
    def chunk_step(k, carry):
        for cc in range(CHUNK):
            c = k * CHUNK + cc
            lanes = slice(cc * BLK, (cc + 1) * BLK)
            y = [ys[pl.ds(t * 8 * CH + c, 8, stride=CH), :] for t in range(4)]
            for i in range(32):
                x = jnp.broadcast_to(xs[pl.ds(i * CH + c, 1), :], (8, BLK))
                row = (i % 8) * 128 + (i // 8) * 32
                for h in range(2):
                    pair = jnp.concatenate([x * y[2 * h], x * y[2 * h + 1]], axis=0)
                    pbuf[row + 16 * h : row + 16 * h + 16, lanes] = pair.astype(bf16)
            for t in range(4):
                pair = jnp.concatenate(
                    [
                        vs[pl.ds((2 * t + h) * 8 * CH + c, 8, stride=CH), :]
                        for h in range(2)
                    ],
                    axis=0,
                )
                high = pair.astype(bf16)
                low = (pair - high.astype(f32)).astype(bf16)
                vbuf[16 * t : 16 * t + 16, lanes] = high
                vbuf[64 + 16 * t : 64 + 16 * t + 16, lanes] = low
        part = lax.dot_general(
            pbuf[...], vbuf[...], (((1,), (1,)), ((), ())), preferred_element_type=f32
        )

        @pl.when(k == 0)
        def _():
            acc[...] = part

        @pl.when(k > 0)
        def _():
            acc[...] = acc[...] + part

        return carry

    lax.fori_loop(0, CH // CHUNK, chunk_step, 0)
    for n in range(8):
        flipped = acc[n * 128 : (n + 1) * 128, :].T
        turned[n * 64 : (n + 1) * 64, :] = flipped[:64] + flipped[64:]
    for part in range(2):
        for facet in range(N_FACET):
            put(facet, part, turned[pl.ds(part * 32 + facet, 8, stride=64), :])


def units_kernel(
    owners, corners, cand_vis, cand_coord, out, vis, coord, xs, ys, vs, pbuf, vbuf, acc, turned, sem
):
    f = lax.axis_index("facet")
    q = lax.axis_index("freq")

    def unit(n, carry):
        owner = jnp.where(
            n == 1, LAST, jnp.where(owners[0] == LAST, owners[1], owners[0])
        ).astype(jnp.int32)
        block = jnp.int32(-1)
        for j in range(BPC):
            block = jnp.where(shifted(f, DELTA[j], -1) == owner, j, block)

        @pl.when(block >= 0)
        def _():
            copies = [
                pltpu.make_async_copy(cand_vis.at[block], vis, sem.at[0]),
                pltpu.make_async_copy(cand_coord.at[block], coord, sem.at[1]),
            ]
            for c in copies:
                c.start()
            for c in copies:
                c.wait()
            prepare_unit(
                q, vis, coord, corners[0, owner, block], corners[1, owner, block], xs, ys, vs
            )

            def put(facet, part, value):
                out[n, facet, part * 8 : (part + 1) * 8, :] = value

            unit_products(xs, ys, vs, pbuf, vbuf, acc, turned, put)

        return carry

    lax.fori_loop(0, 2, unit, 0)


def unit_scratch():
    return [
        pltpu.VMEM((32 * CH, BLK), f32),
        pltpu.VMEM((32 * CH, BLK), f32),
        pltpu.VMEM((64 * CH, BLK), f32),
        pltpu.VMEM((1024, CHUNK * BLK), bf16),
        pltpu.VMEM((128, CHUNK * BLK), bf16),
        pltpu.VMEM((1024, 128), f32),
        pltpu.VMEM((512, 128), f32),
    ]


def units(owners, corners, cand_vis, cand_coord):
    return pl.pallas_call(
        units_kernel,
        out_shape=jax.ShapeDtypeStruct((2, N_FACET, 16, 128), f32),
        in_specs=[pl.BlockSpec(memory_space=pltpu.SMEM)] * 2
        + [pl.BlockSpec(memory_space=pl.ANY)] * 2,
        out_specs=pl.BlockSpec(memory_space=pltpu.VMEM),
        scratch_shapes=[pltpu.VMEM((2, CH, BLK), f32), pltpu.VMEM((3, BLK), f32)]
        + unit_scratch()
        + [pltpu.SemaphoreType.DMA((2,))],
        name="grid_blocks",
    )(owners, corners, cand_vis, cand_coord)


def collect_kernel(res, out, from_a, from_b, total, send_sem, recv_a, recv_b, peer_send, peer_recv):
    f = lax.axis_index("facet")
    q = lax.axis_index("freq")
    x = f % 4
    last_block = jnp.int32(-1)
    for j in range(BPC):
        last_block = jnp.where(f == LAST_POS[j], j, last_block)
    is_last = last_block >= 0
    q_last = last_block % 4
    barrier = pltpu.get_barrier_semaphore()

    def signal(facet, freq):
        pl.semaphore_signal(barrier, inc=1, device_id=(facet, freq), device_id_type=MESH)

    def tell_a(n, carry):
        facet, freq = (n // 4) * 4 + q, n % 4

        @pl.when(jnp.logical_or(facet != f, freq != q))
        def _():
            signal(facet, freq)

        return carry

    lax.fori_loop(0, 32, tell_a, 0)
    for j in range(BPC):
        for freq in range(N_FREQ):

            @pl.when(
                jnp.logical_and(j % 4 == q, jnp.logical_or(f != LAST_POS[j], freq != q))
            )
            def _():
                signal(LAST_POS[j], freq)

    for d in range(1, N_FREQ):
        signal(f, (q + d) % N_FREQ)
    expected = 32 + 3 - jnp.where(x == q, 1, 0)
    expected = expected + jnp.where(is_last, 32 - jnp.where(q_last == q, 1, 0), 0)
    pl.semaphore_wait(barrier, expected)

    def copy_a(facet):
        return pltpu.make_async_remote_copy(
            src_ref=res.at[0, facet],
            dst_ref=from_a.at[f // 4, q],
            send_sem=send_sem.at[0, facet],
            recv_sem=recv_a.at[f // 4, q],
            device_id=(facet, x),
            device_id_type=MESH,
        )

    def copy_b(facet):
        return pltpu.make_async_remote_copy(
            src_ref=res.at[1, facet],
            dst_ref=from_b.at[last_block // 4, q],
            send_sem=send_sem.at[1, facet],
            recv_sem=recv_b.at[last_block // 4, q],
            device_id=(facet, q_last),
            device_id_type=MESH,
        )

    own_a = pltpu.make_async_copy(res.at[0, f], from_a.at[f // 4, q], recv_a.at[f // 4, q])
    own_b = pltpu.make_async_copy(
        res.at[1, f], from_b.at[last_block // 4, q], recv_b.at[last_block // 4, q]
    )

    def send_all(copy, own, to):
        def step(n, carry):
            facet = (f + n) % N_FACET
            here = jnp.logical_and(facet == f, to == q)

            @pl.when(jnp.logical_not(here))
            def _():
                copy(facet).start()

            @pl.when(here)
            def _():
                own.start()

            return carry

        lax.fori_loop(0, N_FACET, step, 0)

    def drain(copy, to):
        def step(facet, carry):
            @pl.when(jnp.logical_not(jnp.logical_and(facet == f, to == q)))
            def _():
                copy(facet).wait_send()

            return carry

        lax.fori_loop(0, N_FACET, step, 0)

    @pl.when(is_last)
    def _():
        send_all(copy_b, own_b, q_last)

    send_all(copy_a, own_a, x)

    def add_a(s, carry):
        for p in range(N_FREQ):
            pltpu.make_async_copy(from_a.at[s, p], from_a.at[s, p], recv_a.at[s, p]).wait()
        total[s] = (from_a[s, 0] + from_a[s, 1]) + (from_a[s, 2] + from_a[s, 3])
        return carry

    lax.fori_loop(0, 8, add_a, 0)
    for s in range(3):

        @pl.when(q + 4 * s < BPC)
        def _():
            for p in range(N_FREQ):
                pltpu.make_async_copy(from_b.at[s, p], from_b.at[s, p], recv_b.at[s, p]).wait()
            total[8 + s] = (from_b[s, 0] + from_b[s, 1]) + (from_b[s, 2] + from_b[s, 3])

    peers = []
    for d in range(1, N_FREQ):
        peers.append(
            pltpu.make_async_remote_copy(
                src_ref=total,
                dst_ref=out.at[q],
                send_sem=peer_send.at[d],
                recv_sem=peer_recv.at[d],
                device_id=(f, (q + d) % N_FREQ),
                device_id_type=MESH,
            )
        )
        peers[-1].start()
    mine = pltpu.make_async_copy(total, out.at[q], peer_send.at[0])
    mine.start()
    mine.wait()
    for d in range(1, N_FREQ):
        source = (q + N_FREQ - d) % N_FREQ
        pltpu.make_async_copy(total, out.at[source], peer_recv.at[d]).wait()
    for p in peers:
        p.wait_send()
    drain(copy_a, x)

    @pl.when(is_last)
    def _():
        drain(copy_b, q_last)


def collect(res):
    return pl.pallas_call(
        collect_kernel,
        out_shape=jax.ShapeDtypeStruct((N_FREQ, SLOTS, 16, 128), f32),
        in_specs=[pl.BlockSpec(memory_space=pl.ANY)],
        out_specs=pl.BlockSpec(memory_space=pl.ANY),
        scratch_shapes=[
            pltpu.VMEM((8, N_FREQ, 16, 128), f32),
            pltpu.VMEM((3, N_FREQ, 16, 128), f32),
            pltpu.VMEM((SLOTS, 16, 128), f32),
            pltpu.SemaphoreType.DMA((2, N_FACET)),
            pltpu.SemaphoreType.DMA((8, N_FREQ)),
            pltpu.SemaphoreType.DMA((3, N_FREQ)),
            pltpu.SemaphoreType.DMA((N_FREQ,)),
            pltpu.SemaphoreType.DMA((N_FREQ,)),
        ],
        compiler_params=pltpu.CompilerParams(collective_id=1, has_side_effects=True),
        name="collect_results",
    )(res)


def split(a):
    high = a.astype(bf16)
    return high, (a - high.astype(f32)).astype(bf16)


def image_kernel(
    owners, corners, assign, counts, got, table, table_t, out, weight, zr, zi, br, bi
):
    q = lax.axis_index("freq")
    lane = lax.broadcasted_iota(jnp.int32, (8, 128), 1)
    first_last = owners[0] == LAST
    other = jnp.where(first_last, owners[1], owners[0]).astype(jnp.int32)
    for b in range(2 * BPC):
        weight[b] = 0.0
    count = counts[0]
    for n in range(2 * BPC):
        weight[assign[0, n]] = jnp.where(n < count, 1.0, 0.0).astype(f32)
    corner_u, corner_v, weights, places = [], [], [], []
    for k in range(2 * BPC):
        j = k % BPC
        if k < BPC:
            owner = jnp.int32(LAST)
            places.append(jnp.int32((j % 4) * SLOTS + 8 + j // 4))
            base = jnp.where(first_last, 0, BPC)
        else:
            owner = other
            t = shifted(other, DELTA[j], 1)
            places.append((t % 4) * SLOTS + t // 4)
            base = jnp.where(first_last, BPC, 0)
        corner_u.append(corners[0, owner, j])
        corner_v.append(corners[1, owner, j])
        weights.append(weight[base + j])
    sine_lane = lane % 32 >= 16
    group = lane // 32
    for tile in range(5):
        parts = [[None] * 4, [None] * 4]
        for g in range(4):
            k = tile * 4 + g
            block = got[places[k]]
            re, im = block[:8] * weights[k], block[8:] * weights[k]
            for half in range(2):
                if half == 0:
                    new_re = jnp.where(sine_lane, -im, re)
                    new_im = jnp.where(sine_lane, re, im)
                else:
                    new_re = jnp.where(sine_lane, -re, -im)
                    new_im = jnp.where(sine_lane, -im, re)
                for i4 in (2 * half, 2 * half + 1):
                    shift = ((g - i4) * 32) % 128
                    for p, value in enumerate((new_re, new_im)):
                        if shift:
                            value = pltpu.roll(value, shift, 1)
                        old = parts[p][i4]
                        parts[p][i4] = value if old is None else jnp.where(group == g, value, old)
        for i4 in range(4):
            zr[i4 * 8 : (i4 + 1) * 8, tile * 128 : (tile + 1) * 128] = parts[0][i4]
            zi[i4 * 8 : (i4 + 1) * 8, tile * 128 : (tile + 1) * 128] = parts[1][i4]
    d_high, d_low = split(table[pl.ds(pl.multiple_of(q * 128, 128), 128), :])

    def apply(z):
        high, low = split(z)
        dot = functools.partial(jnp.dot, preferred_element_type=f32)
        return dot(d_high, high) + (dot(d_high, low) + dot(d_low, high))

    t_re, t_im = apply(zr[...]), apply(zi[...])

    def lanes_of(values):
        tiles = []
        one = lax.broadcasted_iota(jnp.int32, (1, 128), 1) // 32
        for tile in range(5):
            v = jnp.full((1, 128), values[tile * 4], jnp.int32)
            for g in range(1, 4):
                v = jnp.where(one == g, values[tile * 4 + g], v)
            tiles.append(v)
        return jnp.concatenate(tiles, axis=1)

    rows = q * 128 - 256 + lax.broadcasted_iota(jnp.int32, (128, 640), 0)
    turns = jnp.bitwise_and(rows * (2 * lanes_of(corner_u) - 481), 1023)
    p_re, p_im = sincos(turns.astype(f32) * (1.0 / 1024.0))
    l_re = t_re * p_re - t_im * p_im
    l_im = t_re * p_im + t_im * p_re
    columns = lax.broadcasted_iota(jnp.int32, (1, G), 1) - 256
    for k in range(2 * BPC):
        turns = jnp.bitwise_and(columns * (2 * corner_v[k] - 481), 1023)
        c, s = sincos(turns.astype(f32) * (1.0 / 1024.0))
        br[k * 32 : (k + 1) * 32, :] = table_t[...] * c
        bi[k * 32 : (k + 1) * 32, :] = table_t[...] * -s

    def product(a, b):
        ah, al = split(a)
        bh, bl = split(b)
        dot = functools.partial(jnp.dot, preferred_element_type=f32)
        return dot(ah, bh) + (dot(ah, bl) + dot(al, bh))

    out[0] = product(l_re, br[...]) + product(l_im, bi[...])


def image(owners, corners, assign, counts, got):
    d = image_table()
    scale = 1.0 / (SUB * SUB * math.sqrt(2 * BPC * BLK * CHANS))
    smem = pl.BlockSpec(memory_space=pltpu.SMEM)
    vmem = pl.BlockSpec(memory_space=pltpu.VMEM)
    return pl.pallas_call(
        image_kernel,
        out_shape=jax.ShapeDtypeStruct((1, G // N_FREQ, G), f32),
        in_specs=[smem] * 4 + [vmem] * 3,
        out_specs=vmem,
        scratch_shapes=[
            pltpu.SMEM((2 * BPC,), f32),
            pltpu.VMEM((32, 640), f32),
            pltpu.VMEM((32, 640), f32),
            pltpu.VMEM((640, G), f32),
            pltpu.VMEM((640, G), f32),
        ],
        name="make_image",
    )(
        owners,
        corners,
        assign,
        counts,
        got.reshape(N_FREQ * SLOTS, 16, 128),
        jnp.asarray(d * scale, f32),
        jnp.asarray(d.T, f32),
    )


def on_device(visibilities, coords, corners, owners, assign, counts):
    cand_vis, cand_coord = exchange(visibilities, coords)
    res = units(owners, corners, cand_vis, cand_coord)
    got = collect(res)
    return image(owners, corners, assign, counts, got)


def solution(mesh):
    placed = (
        P("facet", None, None, "freq", None),
        P("facet", None, None, None),
        P(),
        P(),
        P("facet", None),
        P("facet"),
    )
    return jax.shard_map(
        on_device, mesh=mesh, in_specs=placed, out_specs=P("facet", "freq", None), check_vma=False
    )
```

time: 719 us -> 53.3 us (0.07); the launches traced: 707 us -> 52.9 us
  waiting for transfers between devices: 388 us -> 0 us
  blocking collectives: 160 us -> 0 us
  Pallas kernels: 0 us -> 50.2 us
  other arithmetic: 47.7 us -> 0 us
  matrix products: 43.7 us -> 0 us
  loops' own time: 31 us -> 0 us
  local copies, waits for them, and re-layouts: 20.8 us -> 2.02 us
  between operations: 16.1 us -> 0.68 us
    reduce_scatter x1 -> x0, waiting for transfers between devices: 227 us -> none  [on_device(): lax.psum_scatter((jnp.dot(cos_table, right_real, precision=highest, prefe...]
    psum x1 -> x0, waiting for transfers between devices: 162 us -> none  [spread(): return lax.psum(kept, axis)]
    psum x1 -> x0, blocking collectives: 160 us -> none  [spread(): return lax.psum(kept, axis)]
    pallas_call x0 -> x4, Pallas kernels: none -> 50.2 us  [the longest x1 31.7 us: collect(): pl.pallas_call(collect_kernel, out_shape=jax.ShapeDtypeStruct((N_FREQ, SL...]
    dot_general x15 -> x0, matrix products: 43.7 us -> none  [the longest x1 6.99 us: on_device(): jnp.dot(sin_table, right_imag, precision=highest, preferred_element_type=...]
    another operation x1 -> x0, other arithmetic: 31.2 us -> none
    another operation x1 -> x0, loops' own time: 31 us -> none  [grid_items(): return lax.fori_loop(0, batch_total, grid_step, initial)]
    dynamic_update_slice x8 -> x0, local copies, waits for them, and re-layouts: 10.8 us -> none  [add_pieces(): lax.dynamic_update_slice(uv_grid, current + pieces[item] * weights[item],...]
  transfers between devices with their start and end apart: 2 -> 0, of which waited for: 2 -> 0; matrix products, arithmetic and copies ran while one was open for 1% -> 0% of each run, Pallas kernels for 0% -> 0%
where the time goes in v1:
time: 53.3 us; the launch traced here: 52.9 us
  Pallas kernels  50.2 us (94%)
  local copies, waits for them, and re-layouts  2.02 us (4%)
  between operations  0.68 us (1%)
    pallas_call x1, Pallas kernels, collect(): pl.pallas_call(collect_kernel, out_shape=jax.ShapeDtypeStruct((N_FREQ, SL...  31.7 us
    pallas_call x1, Pallas kernels, exchange(): pl.pallas_call(exchange_kernel, out_shape=(jax.ShapeDtypeStruct((BPC, 2,...  12.3 us
    pallas_call x1, Pallas kernels, image(): pl.pallas_call(image_kernel, out_shape=jax.ShapeDtypeStruct((1, G // N_FR...  4.09 us
    pallas_call x1, Pallas kernels, units(): pl.pallas_call(units_kernel, out_shape=jax.ShapeDtypeStruct((2, N_FACET,...  2.11 us
    unnamed x4, local copies, waits for them, and re-layouts  2.02 us

profile of v1, /device:TPU:1, one launch (start us, length us, event | category | flops | bytes accessed | tf_op | source)
XLA Modules:
  0.0 52.9 jit_solution(8862528264772140686)
XLA Ops:
  0.0 1.3 %copy.9.coord = f32[1,10,3,128]{3,2,1,0:T(4,128)} copy(f32[1,10,3,128]{3,0,2,1:T(1,128)} %param.9) | data formatting | bytes 30720 | tf_op args[1]
  1.3 0.0 copy-start
  1.3 12.3 %exchange_blocks.1 = (f32[10,2,32,128]{3,2,1,0:T(8,128)}, f32[10,3,128]{2,1,0:T(4,128)}) custom-call(f32[1,10,2,32,128]{4,3,2,1,0:T(8,128)} %vis.1, f32[1,10,3,128]{3,2,1,0:T(4,128)} %copy.9.coord), custom_call_target="tpu_custom_call" | custom-call | tf_op jit(solution)/shard_map/exchange_blocks/pallas_call | solution.py:140
  13.7 0.0 copy-done
  13.7 0.7 %copy.11.corners = s32[2,32,10]{2,1,0:T(8,128)} copy(s32[2,32,10]{1,0,2:T(2,128)S(1)} %copy-done) | data formatting | bytes 5120 | tf_op args[2]
  14.4 2.1 %grid_blocks.1.res = f32[2,32,16,128]{3,2,1,0:T(8,128)} custom-call(s32[2]{0:T(128)} %owners.3, s32[2,32,10]{2,1,0:T(8,128)} %copy.11.corners, f32[10,2,32,128]{3,2,1,0:T(8,128)} %get-tuple-element.7.cand_vis, f32[10,3,128]{2,1,0:T(4,128)} %get-tuple-element.8.cand_coord), custom_call_target="tpu_custom_call" | custom-call | tf_op jit(solution)/shard_map/grid_blocks/pallas_call | solution.py:297
  16.5 31.7 %collect_results.1 = f32[4,11,16,128]{3,2,1,0:T(8,128)} custom-call(f32[2,32,16,128]{3,2,1,0:T(8,128)} %grid_blocks.1.res), custom_call_target="tpu_custom_call" | custom-call | tf_op jit(solution)/shard_map/collect_results/pallas_call | solution.py:451
  48.8 4.1 %make_image.1 = f32[1,128,512]{2,1,0:T(8,128)} custom-call(s32[2]{0:T(128)} %owners.3, s32[2,32,10]{2,1,0:T(8,128)} %copy.11.corners, s32[1,20]{1,0:T(1,128)} %assign.1, s32[1]{0:T(128)S(6)} %copy.12.counts, f32[44,16,128]{2,1,0:T(8,128)} %bitcast.1, f32[512,32]{1,0:T(8,128)} %constant.4.clone.table, f32[32,512]{1,0:T(8,128)} %constant.5.clone.table_t), custom_call_target="tpu_custom_call" | custom-call | tf_op jit(solution)/shard_map/make_image/pallas_call | solution.py:573
Async XLA Ops:
  1.3 12.3 %copy-start = (s32[2,32,10]{1,0,2:T(2,128)S(1)}, s32[2,32,10]{1,0,2:T(2,128)}, u32[]{:S(2)}) copy-start(s32[2,32,10]{1,0,2:T(2,128)} %param.10) | copy-start | bytes 7684
